TPU v7x, 256 devices: a whole 4x4x8 slice. The times are simulated.
256 devices in a mesh: clu: 128 (over z, y, x), rep: 2 (over core).
Axes of the slice: x: 4, y: 4, z: 8, core: 2. Of those that a mesh axis runs over, the one named last changes fastest.
Arguments:
- current: float32 [256, 2, 2, 2048], P('clu', None, 'rep'), may hold values from -6 to 6
- factors: float32 [512, 2, 2, 128, 2048], P(('clu', 'rep')), may hold values from -0.0625 to 0.0625
- ranks: int32 [512], P(('clu', 'rep')), may hold values from 8 to 40
- pair_clusters: int32 [512, 2], replicated, may hold values from 0 to 255, as said below
Outputs:
- field: float32 [256, 2, 2, 2048], P('clu', None, 'rep')
Inputs may be any that keep to these rules, and one draw needn't show every extreme that they name: `pair_clusters`: the 4 cluster ids of the pairs of one device (pairs in blocks of 2 in order) are all different.
All inputs are finite; a program needn't handle non-finite values.
Results may differ from a plain program's by a relative error of at most 0.0003.
Values sent between devices are 32-bit elements; how exact they have to be, the bound alone decides.
A program may use at most 128 MiB of HBM per device.

v0:
```python
import jax
import jax.numpy as jnp
from jax import lax
from jax.sharding import PartitionSpec as P


def project_rows(factor, vector, rank_mask):
    high = lax.Precision.HIGHEST
    real_part = jnp.einsum("prc,pkc->prk", factor[:, 0], vector[:, 0], precision=high) - jnp.einsum(
        "prc,pkc->prk", factor[:, 1], vector[:, 1], precision=high
    )
    imag_part = jnp.einsum("prc,pkc->prk", factor[:, 0], vector[:, 1], precision=high) + jnp.einsum(
        "prc,pkc->prk", factor[:, 1], vector[:, 0], precision=high
    )
    return jnp.stack((real_part, imag_part), axis=1) * rank_mask[:, None, :, None]


def expand_rows(factor, projected):
    high = lax.Precision.HIGHEST
    real_part = jnp.einsum(
        "prc,prk->pkc", factor[:, 0], projected[:, 0], precision=high
    ) - jnp.einsum("prc,prk->pkc", factor[:, 1], projected[:, 1], precision=high)
    imag_part = jnp.einsum(
        "prc,prk->pkc", factor[:, 0], projected[:, 1], precision=high
    ) + jnp.einsum("prc,prk->pkc", factor[:, 1], projected[:, 0], precision=high)
    return jnp.stack((real_part, imag_part), axis=1)


def local(current, factors, ranks, pair_clusters):
    high = lax.Precision.HIGHEST
    clu_count = current.shape[0]
    excitations = current.shape[2] * lax.axis_size("rep")
    unknowns = current.shape[3]
    pair_count = factors.shape[0]
    end_count = 2 * pair_count
    n_rep = lax.axis_size("rep")
    block_index = lax.axis_index("clu") * n_rep + lax.axis_index("rep")
    row_width = 2 * excitations * unknowns
    whole_rhs = lax.all_gather(current, "rep", axis=2, tiled=True)
    flattened = whole_rhs.reshape(clu_count, row_width)
    my_pairs = lax.dynamic_slice_in_dim(pair_clusters, block_index * pair_count, pair_count, 0)
    my_ids = my_pairs.reshape(end_count)
    everything = lax.all_gather(flattened, "clu", axis=0, tiled=True)
    pieces = jnp.take(everything, my_ids, axis=0)
    pieces = pieces.reshape(pair_count, 2, 2, excitations, unknowns)
    left_factor = factors[:, 0]
    right_factor = factors[:, 1]
    rank_mask = (jnp.arange(factors.shape[3], dtype=jnp.int32)[None, :] < ranks[:, None]).astype(
        factors.dtype
    )
    row_terms = expand_rows(left_factor, project_rows(right_factor, pieces[:, 1], rank_mask))
    col_terms = expand_rows(right_factor, project_rows(left_factor, pieces[:, 0], rank_mask))
    contributions = jnp.stack((row_terms, col_terms), axis=1).reshape(end_count, row_width)
    positions = jnp.arange(clu_count * lax.axis_size("clu"), dtype=jnp.int32)
    placer = (positions[:, None] == my_ids[None, :]).astype(jnp.float32)
    summed = lax.psum_scatter(
        jnp.dot(placer, contributions, precision=high), "clu", scatter_dimension=0, tiled=True
    )
    summed = summed.reshape(clu_count, 2, excitations, unknowns)
    return lax.psum_scatter(summed, "rep", scatter_dimension=2, tiled=True)


def solution(mesh):
    placed = (
        P("clu", None, "rep", None),
        P(("clu", "rep"), None, None, None, None),
        P(("clu", "rep")),
        P(),
    )
    return jax.shard_map(
        local, mesh=mesh, in_specs=placed, out_specs=P("clu", None, "rep", None), check_vma=False
    )
```

profile of v0, /device:TPU:1, one launch (start us, length us, event | category | flops | bytes accessed | tf_op | source)
XLA Modules:
  0.0 483.8 jit_solution(11641108925071819487)
XLA Ops:
  7.3 4.7 all_gather.6
  14.7 4.0 fusion.27
  18.7 3.8 copy_bitcast_fusion
  22.5 113.4 %all-gather.3.cloned.1.call-done = f32[128,2,8192]{2,1,0:T(2,128)} async-done(((f32[1,2,8192]{2,1,0:T(2,128)}), f32[128,2,8192]{2,1,0:T(2,128)}) %all-gather.3.cloned.1.call-update) | async-done | bytes 8388624 | tf_op jit(solution)/shard_map/all_gather | solution.py:43
  135.9 10.8 %reshape.87 = f32[256,8192]{1,0:T(8,128)} reshape(f32[128,2,8192]{2,1,0:T(2,128)} %all-gather.3.cloned.1.call-done) | data formatting | bytes 16777216
  146.8 4.0 gather_fusion
  151.2 3.5 fusion.11
  154.7 3.4 fusion.10
  158.1 1.8 fusion.7
  160.0 1.8 fusion.6
  161.8 1.8 fusion.17
  163.6 1.8 fusion.19
  165.5 1.8 fusion.21
  167.3 1.8 fusion.23
  169.2 1.3 fusion.13
  170.5 1.1 fusion.12
  173.8 1.1 fusion.3
  174.9 1.1 fusion.2
  176.0 1.1 fusion.1
  177.1 1.1 fusion
  178.5 5.6 %fusion.24 = f32[256,8192]{1,0:T(8,128)} fusion(f32[4,8192]{1,0:T(4,128)S(1)} %reshape.76, s32[4]{0:T(128)S(1)} %eq.16), kind=kOutput, calls=%fused_computation.38 | convolution fusion | flops 100664320 | bytes 8519696 | tf_op jit(solution)/shard_map/dot_general | solution.py:57
  186.0 258.2 %all-reduce.5.cloned.1.call-done = f32[256,8192]{1,0:T(8,128)} async-done(((f32[256,8192]{1,0:T(8,128)}), f32[256,8192]{1,0:T(8,128)}) %all-reduce.5.cloned.1.call-update) | async-done | bytes 8388624
  446.6 28.6 %all-reduce.7.cloned.1.call-done = f32[2,2,2,2048]{3,1,0,2:T(2,128)} async-done(((f32[2,2,2,2048]{3,1,0,2:T(2,128)}), f32[2,2,2,2048]{3,1,0,2:T(2,128)}) %all-reduce.7.cloned.1.call-update) | async-done | bytes 65552
  475.2 1.4 constant_dynamic-slice_fusion
  (41 shorter events, 10.3 us)
Async XLA Ops:
  6.5 129.4 %all-gather.3.cloned.1.call-start = ((), (), s32[]{:S(2)}) async-start(), calls=%async_computation | async-start | bytes 8454144 | tf_op jit(solution)/shard_map/all_gather | solution.py:43
  12.9 431.4 %all-reduce.5.cloned.1.call-start = ((), (), s32[]{:S(2)}) async-start(), calls=%async_computation.1 | async-start | bytes 16777216
  151.0 7.1 %copy-start = (f32[2,2,128,2048]{3,2,0,1:T(8,128)S(1)}, f32[2,2,128,2048]{3,2,0,1:T(8,128)}, u32[]{:S(2)}) copy-start(f32[2,2,128,2048]{3,2,0,1:T(8,128)} %get-tuple-element.14) | copy-start | bytes 12582916
  151.1 10.7 %copy-start.1 = (f32[2,2,128,2048]{3,2,0,1:T(8,128)S(1)}, f32[2,2,128,2048]{3,2,0,1:T(8,128)}, u32[]{:S(2)}) copy-start(f32[2,2,128,2048]{3,2,0,1:T(8,128)} %get-tuple-element.13) | copy-start | bytes 12582916
  184.1 0.7 copy-start.3
  184.1 261.9 %copy-start.2 = (u32[256]{0:T(256)S(1)}, u32[256]{0:T(256)}, u32[]{:S(2)}) copy-start(u32[256]{0:T(256)} %constant.38) | copy-start | bytes 3076
  184.1 291.0 %all-reduce.7.cloned.1.call-start = ((), (), s32[]{:S(2)}) async-start(), calls=%async_computation.2 | async-start | bytes 131072
Sparse Core Ops, SparseCore 0:
  13.0 122.9 all-gather.2
  184.3 259.8 all-reduce.4
  446.9 28.1 all-reduce.6
where the time goes:
time: 484 us
  waiting for transfers between devices  400 us (83%)
  matrix products  32.6 us (7%)
  local copies, waits for them, and re-layouts  30.4 us (6%)
  between operations  13.9 us (3%)
    unnamed x5, waiting for transfers between devices  287 us
    all_gather x1, waiting for transfers between devices, local(): everything = lax.all_gather(flattened, 'clu', axis=0, tiled=True)  113 us
    unnamed x15, local copies, waits for them, and re-layouts  16.5 us
  transfers between devices with their start and end apart: 3, of which 3 were waited for; matrix products, arithmetic and copies ran while one was open for 2% of the time, Pallas kernels for 0%

commit v1 on v0

--- a/solution.py
+++ b/solution.py
@@ -40,7 +40,9 @@
     flattened = whole_rhs.reshape(clu_count, row_width)
     my_pairs = lax.dynamic_slice_in_dim(pair_clusters, block_index * pair_count, pair_count, 0)
     my_ids = my_pairs.reshape(end_count)
-    everything = lax.all_gather(flattened, "clu", axis=0, tiled=True)
+    everything = jnp.concatenate(
+        lax.all_to_all(jnp.stack([flattened] * lax.axis_size("clu")), "clu", 0, 0), axis=0
+    )
     pieces = jnp.take(everything, my_ids, axis=0)
     pieces = pieces.reshape(pair_count, 2, 2, excitations, unknowns)
     left_factor = factors[:, 0]

time: 484 us -> 565 us (1.17)
  waiting for transfers between devices: 400 us -> 460 us
  starting transfers between devices: 0.09 us -> 14.5 us
  local copies, waits for them, and re-layouts: 30.4 us -> 37.2 us
    all_to_all x0 -> x1, waiting for transfers between devices: none -> 176 us  [local(): lax.all_to_all(jnp.stack([flattened] * lax.axis_size('clu')), 'clu', 0, 0)]
    all_gather x1 -> x0, waiting for transfers between devices: 113 us -> none  [local(): everything = lax.all_gather(flattened, 'clu', axis=0, tiled=True)]
    all_to_all x0 -> x1, starting transfers between devices: none -> 14.4 us  [local(): lax.all_to_all(jnp.stack([flattened] * lax.axis_size('clu')), 'clu', 0, 0)]
    unnamed x15, local copies, waits for them, and re-layouts: 16.5 us -> 4.94 us
    reshape x0 -> x1, local copies, waits for them, and re-layouts: none -> 10.8 us  [local(): jnp.concatenate(lax.all_to_all(jnp.stack([flattened] * lax.axis_size('clu...]
    another operation x0 -> x2, local copies, waits for them, and re-layouts: none -> 7.49 us  [local(): jnp.stack([flattened] * lax.axis_size('clu'))]
    unnamed x5 -> x4, waiting for transfers between devices: 287 us -> 284 us
where the time goes in v1:
time: 565 us; the launch traced here: 564 us
  waiting for transfers between devices  460 us (81%)
  local copies, waits for them, and re-layouts  37.2 us (7%)
  matrix products  32.6 us (6%)
  starting transfers between devices  14.5 us (3%)
  between operations  14.2 us (3%)
    unnamed x4, waiting for transfers between devices  284 us
    all_to_all x1, waiting for transfers between devices, local(): lax.all_to_all(jnp.stack([flattened] * lax.axis_size('clu')), 'clu', 0, 0)  176 us
    all_to_all x1, starting transfers between devices, local(): lax.all_to_all(jnp.stack([flattened] * lax.axis_size('clu')), 'clu', 0, 0)  14.4 us
  transfers between devices with their start and end apart: 3, of which 3 were waited for; matrix products, arithmetic and copies ran while one was open for 2% of the time, Pallas kernels for 0%

profile of v1, /device:TPU:1, one launch (start us, length us, event | category | flops | bytes accessed | tf_op | source)
XLA Modules:
  0.0 564.3 jit_solution(11300845898162896210)
XLA Ops:
  7.3 4.7 all_gather.3
  12.2 7.4 %stack.48 = f32[128,2,8192]{2,1,0:T(2,128)} broadcast(f32[2,8192]{1,0:T(2,128)S(1)} %stack_reshape.2), dimensions={1,2} | broadcast | bytes 8454144 | tf_op jit(solution)/shard_map/stack | solution.py:44
  19.6 14.4 %all-to-all-start = ((f32[128,2,8192]{2,1,0:T(2,128)}), f32[128,2,8192]{2,1,0:T(2,128)}, u32[]{:S(2)}, u32[]{:S(2)}) async-start(f32[128,2,8192]{2,1,0:T(2,128)} %stack.48), calls=%async_computation | async-start | bytes 16777216 | tf_op jit(solution)/shard_map/all_to_all | solution.py:44
  35.2 4.0 fusion.27
  39.3 3.8 copy_bitcast_fusion
  43.1 175.5 %all-to-all-done = f32[128,2,8192]{2,1,0:T(2,128)} async-done(((f32[128,2,8192]{2,1,0:T(2,128)}), f32[128,2,8192]{2,1,0:T(2,128)}, u32[]{:S(2)}, u32[]{:S(2)}) %all-to-all-start) | async-done | bytes 8388640 | tf_op jit(solution)/shard_map/all_to_all | solution.py:44
  218.6 10.8 %reshape.76 = f32[256,8192]{1,0:T(8,128)} reshape(f32[128,2,8192]{2,1,0:T(2,128)} %all-to-all-done) | data formatting | bytes 16777216 | tf_op jit(solution)/shard_map/reshape | solution.py:43
  229.4 4.0 gather_fusion
  233.8 3.5 fusion.11
  237.4 3.4 fusion.10
  240.8 1.8 fusion.7
  242.6 1.8 fusion.6
  244.5 1.8 fusion.17
  246.3 1.8 fusion.19
  248.1 1.8 fusion.21
  250.0 1.8 fusion.23
  251.9 1.3 fusion.13
  256.5 1.1 fusion.3
  257.6 1.1 fusion.2
  258.7 1.1 fusion.1
  261.2 5.6 fusion.24
  268.7 255.7 %all-reduce.5.cloned.1.call-done = f32[256,8192]{1,0:T(8,128)} async-done(((f32[256,8192]{1,0:T(8,128)}), f32[256,8192]{1,0:T(8,128)}) %all-reduce.5.cloned.1.call-update) | async-done | bytes 8388624
  526.8 28.6 %all-reduce.7.cloned.1.call-done = f32[2,2,2,2048]{3,1,0,2:T(2,128)} async-done(((f32[2,2,2,2048]{3,1,0,2:T(2,128)}), f32[2,2,2,2048]{3,1,0,2:T(2,128)}) %all-reduce.7.cloned.1.call-update) | async-done | bytes 65552
  555.4 1.4 constant_dynamic-slice_fusion
  (43 shorter events, 11.2 us)
Async XLA Ops:
  19.6 15.5 %copy-start.2 = (s32[2]{0:T(128)S(1)}, s32[2]{0:T(128)}, u32[]{:S(2)}) copy-start(s32[2]{0:T(128)} %param.6) | copy-start | bytes 28
  19.6 199.0 %all-to-all-start = ((f32[128,2,8192]{2,1,0:T(2,128)}), f32[128,2,8192]{2,1,0:T(2,128)}, u32[]{:S(2)}, u32[]{:S(2)}) async-start(f32[128,2,8192]{2,1,0:T(2,128)} %stack.48), calls=%async_computation | async-start | bytes 16777216 | tf_op jit(solution)/shard_map/all_to_all | solution.py:44
  34.1 490.4 %all-reduce.5.cloned.1.call-start = ((), (), s32[]{:S(2)}) async-start(), calls=%async_computation.1 | async-start | bytes 16777216
  233.6 7.1 %copy-start = (f32[2,2,128,2048]{3,2,0,1:T(8,128)S(1)}, f32[2,2,128,2048]{3,2,0,1:T(8,128)}, u32[]{:S(2)}) copy-start(f32[2,2,128,2048]{3,2,0,1:T(8,128)} %get-tuple-element.14) | copy-start | bytes 12582916
  233.8 10.7 %copy-start.1 = (f32[2,2,128,2048]{3,2,0,1:T(8,128)S(1)}, f32[2,2,128,2048]{3,2,0,1:T(8,128)}, u32[]{:S(2)}) copy-start(f32[2,2,128,2048]{3,2,0,1:T(8,128)} %get-tuple-element.13) | copy-start | bytes 12582916
  266.8 0.7 copy-start.4
  266.8 259.4 %copy-start.3 = (u32[256]{0:T(256)S(1)}, u32[256]{0:T(256)}, u32[]{:S(2)}) copy-start(u32[256]{0:T(256)} %constant.38) | copy-start | bytes 3076
  266.8 288.6 %all-reduce.7.cloned.1.call-start = ((), (), s32[]{:S(2)}) async-start(), calls=%async_computation.2 | async-start | bytes 131072
Sparse Core Ops, SparseCore 0:
  266.9 257.4 all-reduce.4
  527.1 28.1 all-reduce.6
